TPU v7x, 32 devices: a whole 2x2x4 slice. The times are simulated.
32 devices in a mesh: groups: 2 (over x), ctx: 8 (over z, y), exp: 2 (over core).
Axes of the slice: x: 2, y: 2, z: 4, core: 2. Of those that a mesh axis runs over, the one named last changes fastest.
Arguments:
- x_in: bfloat16 [4096, 2048], P(('groups', 'ctx'), 'exp'), parts along dimension 0, may hold values from -6 to 6
- bc_in: bfloat16 [4096, 2, 512], P(('groups', 'ctx'), None, 'exp'), parts along dimension 0, may hold values from -6 to 6
- z_in: bfloat16 [4096, 2048], P(('groups', 'ctx'), 'exp'), parts along dimension 0, may hold values from -6 to 6
- time_step: float32 [4096, 32], P(('groups', 'ctx'), 'exp'), parts along dimension 0, may hold values from 0.002 to 0.02
- decay_log: float32 [4096, 32], P(('groups', 'ctx'), 'exp'), parts along dimension 0, may hold values from -1 to 0
- conv_inner: bfloat16 [4, 2048], P(None, 'exp'), may hold values from -3 to 3
- conv_bc: bfloat16 [4, 2, 512], P(None, None, 'exp'), may hold values from -3 to 3
- skip_gain: float32 [32], P('exp'), may hold values from 0.5 to 1.5
- start_state: bfloat16 [64, 64, 128], P(('groups', 'exp')), parts along dimension 0, may hold values from -3 to 3
- norm_gain: bfloat16 [2048], P('exp'), may hold values from 0.099609375 to 1.8984375
- out_proj: bfloat16 [2048, 2688], P('exp', 'ctx'), may hold values from -0.125 to 0.125
- residual: bfloat16 [4096, 2688], P(('groups', 'ctx', 'exp')), parts along dimension 0, may hold values from -40 to 40
- moe_gain: bfloat16 [2688], replicated, may hold values from 0.099609375 to 1.8984375
- routes: int32 [4096, 6], P(('groups', 'ctx', 'exp')), parts along dimension 0, may hold values from 0 to 15, all different within a row; in each aligned block of 128 rows (0 to 127, 128 to 255, ...) at most 64 rows name the same one
- gate_weight: float32 [4096, 6], P(('groups', 'ctx', 'exp')), parts along dimension 0, may hold values from 0.1 to 0.4
- up_weight: bfloat16 [16, 2688, 928], P(('ctx', 'exp')), may hold values from -0.125 to 0.125
- down_weight: bfloat16 [16, 928, 2688], P(('ctx', 'exp')), may hold values from -0.1875 to 0.1875
Outputs:
- layer_out: bfloat16 [4096, 2688], P(('groups', 'ctx', 'exp')), parts along dimension 0
There are 2 independent parts, one for each index of `groups`. A program takes and returns all parts, laid end to end along the dimension named above; an argument that names none is the same for every part. Nothing has to cross between parts.
Inputs may be any that keep to these rules, and one draw needn't show every extreme that they name: `routes`: each row names 6 different experts; among the rows of one device (aligned blocks of 128 rows) no expert is named more than 64 times.
All inputs are finite; a program needn't handle non-finite values.
Results may differ from a plain program's by a relative error of at most 0.0056.
Values may be sent and summed in bfloat16 or wider, within the bound.
No kernel may reach another device: no remote copies, remote signals or barrier semaphores. Data moves between devices by JAX's collectives and lax.ppermute only.
A program may use at most 128 MiB of HBM per device.

v0:
```python
import jax
import jax.numpy as jnp
from jax import lax
from jax.sharding import PartitionSpec as P

HEAD_DIM = 64
STATE = 128
KERNEL = 4
EPS = 1e-05
HIGH = lax.Precision.HIGHEST


def from_behind(array, axis, by):
    count = lax.axis_size(axis)
    pairs = [(i, i + by) for i in range(count) if 0 <= i + by < count]
    return lax.ppermute(array, axis, pairs)


def carried_in(array, axis, combine, identity):
    count, index = (lax.axis_size(axis), lax.axis_index(axis))
    everything = jax.tree.map(lambda part: lax.all_gather(part, axis), array)
    start = jax.tree.map(
        lambda part, zero: jnp.broadcast_to(jnp.asarray(zero, part.dtype), part.shape),
        array,
        identity,
    )

    def hop(k, before):
        reached = k < index
        new = combine(before, jax.tree.map(lambda part: part[k], everything))
        return jax.tree.map(lambda a, b: jnp.where(reached, a, b), new, before)

    return lax.fori_loop(0, count, hop, start)


def causal_conv(sequence, previous, taps):
    length = sequence.shape[0]
    padded = jnp.concatenate([previous, sequence], 0).astype(jnp.float32)
    summed = jnp.zeros(sequence.shape, jnp.float32)
    for offset in range(taps.shape[0]):
        summed = summed + taps[offset].astype(jnp.float32) * padded[offset : offset + length]
    return jax.nn.silu(summed).astype(jnp.bfloat16)


def chain_pair(earlier, later):
    return (earlier[0] * later[0], later[0][..., None, None] * earlier[1] + later[1])


def per_device(
    x_in,
    bc_in,
    z_in,
    time_step,
    decay_log,
    conv_inner,
    conv_bc,
    skip_gain,
    start_state,
    norm_gain,
    out_proj,
    residual,
    moe_gain,
    routes,
    gate_weight,
    up_weight,
    down_weight,
):
    block_len = x_in.shape[0]
    local_heads = time_step.shape[1]
    local_groups = bc_in.shape[2] // STATE
    per_group = local_heads // local_groups
    rim_rows = KERNEL - 1
    prev_inner, prev_bc = from_behind(
        (x_in[block_len - rim_rows :], bc_in[block_len - rim_rows :]), "ctx", 1
    )
    inner_act = causal_conv(x_in, prev_inner, conv_inner)
    bc_act = causal_conv(bc_in, prev_bc, conv_bc)
    values = inner_act.astype(jnp.float32).reshape(block_len, local_groups, per_group, HEAD_DIM)
    b_rows = bc_act[:, 0].astype(jnp.float32).reshape(block_len, local_groups, STATE)
    c_rows = bc_act[:, 1].astype(jnp.float32).reshape(block_len, local_groups, STATE)
    log_steps = decay_log.reshape(block_len, local_groups, per_group)
    step_sizes = time_step.reshape(block_len, local_groups, per_group)
    cumulative = jnp.cumsum(log_steps, axis=0)
    block_log = cumulative[block_len - 1]
    to_end = jnp.exp(block_log[None] - cumulative) * step_sizes
    end_state = jnp.einsum("tgrp,tgn->grpn", to_end[..., None] * values, b_rows, precision=HIGH)
    block_decay = jnp.exp(block_log)
    prior_decay, prior_state = carried_in(
        (block_decay, end_state),
        "ctx",
        chain_pair,
        (jnp.ones_like(block_decay), jnp.zeros_like(end_state)),
    )
    entering = (
        prior_decay[..., None, None]
        * start_state.astype(jnp.float32).reshape(local_groups, per_group, HEAD_DIM, STATE)
        + prior_state
    )
    carried = jnp.exp(cumulative)[..., None] * jnp.einsum(
        "tgn,grpn->tgrp", c_rows, entering, precision=HIGH
    )
    scores = jnp.einsum("tgn,sgn->tsg", c_rows, b_rows, precision=HIGH)
    position = jnp.arange(block_len)
    causal = (position[:, None] >= position[None, :])[:, :, None, None]
    spread_log = cumulative[:, None] - cumulative[None, :]
    decay_table = jnp.where(causal, jnp.exp(jnp.where(causal, spread_log, 0.0)), 0.0)
    mix_table = decay_table * step_sizes[None] * scores[..., None]
    local_part = jnp.einsum("tsgr,sgrp->tgrp", mix_table, values, precision=HIGH)
    outputs = (
        carried + local_part + skip_gain.reshape(local_groups, per_group)[None, :, :, None] * values
    )
    gated = outputs.reshape(block_len, local_groups, -1) * jax.nn.silu(
        z_in.astype(jnp.float32).reshape(block_len, local_groups, -1)
    )
    mean_square = jnp.mean(gated * gated, axis=-1, keepdims=True)
    normed = (
        (
            gated
            * lax.rsqrt(mean_square + EPS)
            * norm_gain.astype(jnp.float32).reshape(local_groups, -1)
        )
        .reshape(block_len, -1)
        .astype(jnp.bfloat16)
    )
    partial_out = jnp.dot(
        normed,
        lax.all_gather(out_proj, "ctx", axis=1, tiled=True),
        preferred_element_type=jnp.float32,
    )
    mixed = lax.psum_scatter(partial_out, "exp", scatter_dimension=0, tiled=True)
    hidden_f = (residual.astype(jnp.float32) + mixed).astype(jnp.bfloat16).astype(jnp.float32)
    expert_in = (
        hidden_f
        * lax.rsqrt(jnp.mean(hidden_f * hidden_f, axis=-1, keepdims=True) + EPS)
        * moe_gain.astype(jnp.float32)
    ).astype(jnp.bfloat16)
    tok_rows = routes.shape[0]
    top_count = routes.shape[1]
    model_width = expert_in.shape[1]
    ctx_count = lax.axis_size("ctx")
    exp_count = lax.axis_size("exp")
    experts = ctx_count * exp_count * up_weight.shape[0]
    capacity = max(2, 4 * tok_rows * top_count // (3 * experts))
    flat_ids = routes.reshape(-1)
    one_hot = (flat_ids[:, None] == jnp.arange(experts, dtype=jnp.int32)[None, :]).astype(jnp.int32)
    ranks = jnp.cumsum(one_hot, axis=0) - 1
    slots = jnp.sum(one_hot * ranks, axis=1)
    source_rows = jnp.repeat(jnp.arange(tok_rows, dtype=jnp.int32), top_count)
    send_buffer = (
        jnp.zeros((experts, capacity, model_width), jnp.bfloat16)
        .at[flat_ids, slots]
        .set(expert_in[source_rows])
    )
    arrived = lax.all_to_all(send_buffer, ("ctx", "exp"), split_axis=0, concat_axis=0, tiled=True)
    leading = arrived.shape[:-1]
    flat_rows = arrived.reshape(-1, arrived.shape[-1])
    inner = jnp.dot(flat_rows, up_weight[0], preferred_element_type=jnp.float32)
    inner = jnp.square(jax.nn.relu(inner)).astype(jnp.bfloat16)
    layer_answer = jnp.dot(inner, down_weight[0], preferred_element_type=jnp.float32).astype(
        jnp.bfloat16
    )
    finished = layer_answer.reshape(leading + (arrived.shape[-1],))
    returned = lax.all_to_all(finished, ("ctx", "exp"), split_axis=0, concat_axis=0, tiled=True)
    gathered = returned[flat_ids, slots].reshape(tok_rows, top_count, model_width)
    combined = jnp.sum(gate_weight[..., None] * gathered.astype(jnp.float32), axis=1)
    return (hidden_f + combined).astype(jnp.bfloat16)


def solution(mesh):
    in_specs = (
        P(("groups", "ctx"), "exp"),
        P(("groups", "ctx"), None, "exp"),
        P(("groups", "ctx"), "exp"),
        P(("groups", "ctx"), "exp"),
        P(("groups", "ctx"), "exp"),
        P(None, "exp"),
        P(None, None, "exp"),
        P("exp"),
        P(("groups", "exp"), None, None),
        P("exp"),
        P("exp", "ctx"),
        P(("groups", "ctx", "exp"), None),
        P(),
        P(("groups", "ctx", "exp"), None),
        P(("groups", "ctx", "exp"), None),
        P(("ctx", "exp"), None, None),
        P(("ctx", "exp"), None, None),
    )
    out_specs = P(("groups", "ctx", "exp"), None)
    return jax.shard_map(
        per_device, mesh=mesh, in_specs=in_specs, out_specs=out_specs, check_vma=False
    )
```

profile of v0, /device:TPU:13, one launch (start us, length us, event | category | flops | bytes accessed | tf_op | source)
XLA Modules:
  0.0 684.6 jit_solution(16131043887685088930)
XLA Ops:
  6.5 0.7 slice.88
  7.5 3.1 collective-permute-start.1
  10.6 0.7 slice.79
  11.4 3.1 collective-permute-start
  14.5 0.9 slice_convert_fusion.3
  15.4 1.2 reduce-window.14
  17.0 0.6 slice_bitcast_fusion
  17.6 0.9 copy.94
  18.8 0.7 bitcast_convert_fusion.3
  19.5 1.1 copy.98
  20.9 0.8 multiply_convert_fusion.4
  21.7 0.7 fusion.53
  22.6 0.6 multiply_convert_fusion.2
  23.4 1.5 fusion.29
  25.0 0.7 all-gather.4.cloned.1.call-update
  26.2 0.6 convert_element_type.82
  26.8 10.8 %all_gather.13 = f32[8,2,8]{2,1,0:T(2,128)S(1)} all-gather(f32[1,2,8]{2,1,0:T(2,128)S(1)} %copy-done.10), channel_id=1, replica_groups=mesh['groups'=2,'ctx'=8,'exp'=2] {'ctx'}, dimensions={0}, use_global_device_ids=true | all-gather | bytes 576 | tf_op jit(solution)/shard_map/all_gather | solution.py:21
  37.6 1.2 convolution_bitcast_fusion.1
  38.8 1.0 copy.105
  39.8 5.4 fusion.23
  45.2 51.4 %all-gather.6.cloned.1.call-done = f32[16,8,64,128]{3,2,1,0:T(8,128)} async-done(((f32[2,8,64,128]{3,2,1,0:T(8,128)}), f32[16,8,64,128]{3,2,1,0:T(8,128)}) %all-gather.6.cloned.1.call-update) | async-done | bytes 4194320 | tf_op jit(solution)/shard_map/all_gather | solution.py:21
  96.6 9.7 %while.16 = (s32[]{:T(128)}, f32[2,8]{1,0:T(2,128)S(1)}, f32[2,8,64,128]{3,2,1,0:T(8,128)S(1)}, s32[]{:T(128)}, f32[8,2,8]{2,1,0:T(2,128)S(1)}, /*index=5*/f32[8,2,8,64,128]{4,3,2,1,0:T(8,128)}, s32[]{:T(128)}, s32[]{:T(128)}) while((s32[]{:T(128)}, f32[2,8]{1,0:T(2,128)S(1)}, f32[2,8,64,128]{3,2,1,0:T(8,128)S(1)}, s32[]{:T(128)}, ...), condition=%wide.region_3.4_spmd.clone, body=%wide.region_2.3_spmd.clone.sunk | while | flops 524340 | bytes 1573299 | solution.py:33
  96.6 1.2 fusion.72
  97.8 1.2 fusion.72
  99.0 1.2 fusion.72
  100.2 1.2 fusion.72
  101.4 1.2 fusion.72
  102.7 1.2 fusion.72
  103.9 1.2 fusion.72
  105.1 1.2 fusion.72
  106.3 3.2 multiply_reduce_fusion.1
  110.2 1.6 copy.106
  111.8 74.2 %all-gather.4.cloned.1.call-done = bf16[1024,2688]{0,1:T(8,128)(2,1)} async-done(((bf16[1024,336]{0,1:T(8,128)(2,1)}), bf16[1024,2688]{0,1:T(8,128)(2,1)}) %all-gather.4.cloned.1.call-update) | async-done | bytes 5505040 | tf_op jit(solution)/shard_map/all_gather | solution.py:127
  186.0 6.1 fusion.33
  192.9 1.7 reduce-window.16
  195.0 9.6 %reduce-scatter.2.cloned.1.call-done = f32[128,2688]{1,0:T(8,128)} async-done(((f32[256,2688]{1,0:T(8,128)}), f32[128,2688]{1,0:T(8,128)}) %reduce-scatter.2.cloned.1.call-update) | async-done | bytes 1376272 | tf_op jit(solution)/shard_map/reduce_scatter | solution.py:130
  204.6 1.6 fusion.19
  206.5 4.9 gather_fusion
  211.4 3.0 broadcast_in_dim.27
  214.3 158.3 %scatter_fusion = bf16[16,64,2688]{2,1,0:T(8,128)(2,1)} fusion(bf16[16,64,2688]{2,1,0:T(8,128)(2,1)} %broadcast_in_dim.27, s32[768]{0:T(1024)S(1)} %get-tuple-element.151, bf16[768,2688]{1,0:T(8,128)(2,1)} %gather_fusion), kind=kCustom, calls=%fused_computation.2 | custom fusion | bytes 12392448 | tf_op jit(solution)/shard_map/scatter | solution.py:152
  372.6 126.7 %all_to_all.10 = bf16[16,64,2688]{2,1,0:T(8,128)(2,1)} all-to-all(bf16[16,64,2688]{2,1,0:T(8,128)(2,1)} %scatter_fusion), channel_id=1, replica_groups=mesh['groups'=2,'ctx'=8,'exp'=2] {'ctx','exp'}, dimensions={0} | all-to-all | bytes 11010048 | tf_op jit(solution)/shard_map/all_to_all | solution.py:154
  499.3 18.8 %convolution_convert_fusion = bf16[1024,2688]{1,0:T(8,128)(2,1)} fusion(bf16[1,928,2688]{2,1,0:T(8,128)(2,1)} %param.35, bf16[1024,2688]{1,0:T(8,128)(2,1)} %bitcast.116, bf16[1,2688,928]{1,2,0:T(8,128)(2,1)} %param.34), kind=kOutput, calls=%fused_computation.8 | convolution fusion | flops 10222927872 | bytes 20987904 | tf_op jit(solution)/shard_map/dot_general | solution.py:159
  518.1 5.6 all-to-all-start.1
  523.9 120.5 %all-to-all-done.1 = bf16[16,64,2688]{2,1,0:T(8,128)(2,1)} async-done(((bf16[16,64,2688]{2,1,0:T(8,128)(2,1)}), bf16[16,64,2688]{2,1,0:T(8,128)(2,1)}, u32[]{:S(2)}, u32[]{:S(2)}) %all-to-all-start.1) | async-done | bytes 5505056 | tf_op jit(solution)/shard_map/all_to_all | solution.py:163
  644.3 16.7 %gather_fusion.1 = bf16[768,2688]{1,0:T(8,128)(2,1)} fusion(bf16[16,64,2688]{2,1,0:T(8,128)(2,1)} %all-to-all-done.1, s32[768]{0:T(1024)S(1)} %get-tuple-element.150), kind=kCustom, calls=%fused_computation.1 | custom fusion | bytes 8263680 | tf_op jit(solution)/shard_map/gather | solution.py:164
  661.0 7.9 %reshape.218 = f32[128,6,2688]{2,1,0:T(8,128)} reshape(bf16[768,2688]{1,0:T(8,128)(2,1)} %gather_fusion.1) | data formatting | bytes 12386304 | tf_op jit(solution)/shard_map/convert_element_type | solution.py:165
  668.9 8.1 %multiply_reduce_fusion = f32[128,2688]{1,0:T(8,128)S(1)} fusion(f32[128,6,2688]{2,1,0:T(8,128)} %reshape.218, f32[128,6]{1,0:T(8,128)S(1)} %copy.109), kind=kLoop, calls=%fused_computation.7 | loop fusion | flops 3784704 | bytes 9636864 | tf_op jit(solution)/shard_map/reduce_sum | solution.py:165
  677.1 1.0 fusion.22
  (87 shorter events, 4.6 us)
Async XLA Ops:
  6.5 8.8 %copy-start = (f32[256,16]{0,1:T(8,128)S(1)}, f32[256,16]{0,1:T(8,128)}, u32[]{:S(2)}) copy-start(f32[256,16]{0,1:T(8,128)} %param.23) | copy-start | bytes 49156
  6.5 15.8 %copy-start.3 = (bf16[256,1024]{1,0:T(8,128)(2,1)S(1)}, bf16[256,1024]{1,0:T(8,128)(2,1)}, u32[]{:S(2)}) copy-start(bf16[256,1024]{1,0:T(8,128)(2,1)} %param.19) | copy-start | bytes 1572868
  6.5 90.0 %all-gather.6.cloned.1.call-start = ((), (), s32[]{:S(2)}) async-start(), calls=%async_computation.5 | async-start | bytes 4718592 | tf_op jit(solution)/shard_map/all_gather | solution.py:21
  7.5 13.2 %collective-permute-start.1 = (bf16[3,2,256]{0,2,1:T(8,128)(2,1)S(1)}, bf16[3,2,256]{0,2,1:T(8,128)(2,1)S(1)}, u32[]{:S(2)}, u32[]{:S(2)}) collective-permute-start(bf16[3,2,256]{0,2,1:T(8,128)(2,1)S(1)} %copy.97), channel_id=1, source_target_pairs={{0,2},{2,4},{4,6},{6,8},{8,10},{10,12},{12,14},{1,3},{3,5},{5,7},{... | collective-permute-start | bytes 9224 | tf_op jit(solution)/shard_map/ppermute | solution.py:16
  11.4 11.0 %collective-permute-start = (bf16[3,1024]{1,0:T(4,128)(2,1)S(1)}, bf16[3,1024]{1,0:T(4,128)(2,1)S(1)}, u32[]{:S(2)}, u32[]{:S(2)}) collective-permute-start(bf16[3,1024]{1,0:T(4,128)(2,1)S(1)} %slice.79), channel_id=1, source_target_pairs={{0,2},{2,4},{4,6},{6,8},{8,10},{10,12},{12,14},{1,3},{3,5},{5,7},{... | collective-permute-start | bytes 18440 | tf_op jit(solution)/shard_map/ppermute | solution.py:16
  22.5 3.4 copy-start.4
  22.5 3.6 copy-start.14
  22.5 3.7 copy-start.12
  22.6 4.3 copy-start.10
  23.4 16.4 %copy-start.6 = (f32[256,16]{0,1:T(8,128)S(1)}, f32[256,16]{0,1:T(8,128)}, u32[]{:S(2)}) copy-start(f32[256,16]{0,1:T(8,128)} %param.22) | copy-start | bytes 49156
  24.9 161.1 %all-gather.4.cloned.1.call-start = ((), (), s32[]{:S(2)}) async-start(), calls=%async_computation.3 | async-start | bytes 6193152 | tf_op jit(solution)/shard_map/all_gather | solution.py:127
  25.7 178.9 %reduce-scatter.2.cloned.1.call-start = ((), (), s32[]{:S(2)}) async-start(), calls=%async_computation.4 | async-start | bytes 4128768 | tf_op jit(solution)/shard_map/reduce_scatter | solution.py:130
  45.2 61.1 %copy-start.5 = (bf16[256,1,256]{0,2,1:T(8,128)(2,1)S(1)}, bf16[256,1,256]{0,2,1:T(8,128)(2,1)}, u32[]{:S(2)}) copy-start(bf16[256,1,256]{0,2,1:T(8,128)(2,1)} %get-tuple-element.172) | copy-start | bytes 393220
  45.2 61.1 %copy-start.13 = (bf16[16,64,128]{2,1,0:T(8,128)(2,1)S(1)}, bf16[16,64,128]{2,1,0:T(8,128)(2,1)}, u32[]{:S(2)}) copy-start(bf16[16,64,128]{2,1,0:T(8,128)(2,1)} %param.27) | copy-start | bytes 786436
  109.5 76.5 %copy-start.11 = (f32[1024]{0:T(1024)S(1)}, f32[1024]{0:T(1024)}, u32[]{:S(2)}) copy-start(f32[1024]{0:T(1024)} %convert_element_type.82) | copy-start | bytes 12292
  186.0 6.1 copy-start.8
  186.0 6.7 copy-start.7
  186.0 18.6 %copy-start.2 = (bf16[128,2688]{1,0:T(8,128)(2,1)S(1)}, bf16[128,2688]{1,0:T(8,128)(2,1)}, u32[]{:S(2)}) copy-start(bf16[128,2688]{1,0:T(8,128)(2,1)} %param.30) | copy-start | bytes 2064388
  518.1 5.6 copy-start.9
  518.1 126.2 %all-to-all-start.1 = ((bf16[16,64,2688]{2,1,0:T(8,128)(2,1)}), bf16[16,64,2688]{2,1,0:T(8,128)(2,1)}, u32[]{:S(2)}, u32[]{:S(2)}) async-start(bf16[16,64,2688]{2,1,0:T(8,128)(2,1)} %bitcast.115), calls=%async_computation.2 | async-start | bytes 11010048 | tf_op jit(solution)/shard_map/all_to_all | solution.py:163
  668.9 9.1 %copy-start.1 = (f32[256,16]{0,1:T(8,128)S(1)}, f32[256,16]{0,1:T(8,128)}, u32[]{:S(2)}) copy-start(f32[256,16]{0,1:T(8,128)} %param.23) | copy-start | bytes 49156
Sparse Core Ops, SparseCore 0:
  25.0 71.4 all-gather.5
  98.7 87.2 all-gather.3
  192.2 12.3 reduce-scatter.1
where the time goes:
time: 688 us; the launch traced here: 685 us
  waiting for transfers between devices  256 us (37%)
  local copies, waits for them, and re-layouts  201 us (29%)
  blocking collectives  137 us (20%)
  matrix products  36.1 us (5%)
  other arithmetic  27.9 us (4%)
  between operations  13.5 us (2%)
  starting transfers between devices  12 us (2%)
    scatter x1, local copies, waits for them, and re-layouts, per_device(): send_buffer = jnp.zeros((experts, capacity, model_width), jnp.bfloat16).a...  158 us
    all_to_all x1, blocking collectives, per_device(): lax.all_to_all(send_buffer, ('ctx', 'exp'), split_axis=0, concat_axis=0,...  127 us
    all_to_all x1, waiting for transfers between devices, per_device(): lax.all_to_all(finished, ('ctx', 'exp'), split_axis=0, concat_axis=0, til...  120 us
    all_gather x1, waiting for transfers between devices, per_device(): lax.all_gather(out_proj, 'ctx', axis=1, tiled=True)  74.2 us
    all_gather x1, waiting for transfers between devices, carried_in(): everything = jax.tree.map(lambda part: lax.all_gather(part, axis), array)  51.4 us
    dot_general x1, matrix products, per_device(): jnp.dot(inner, down_weight[0], preferred_element_type=jnp.float32)  18.8 us
    gather x1, local copies, waits for them, and re-layouts, per_device(): returned[flat_ids, slots].reshape(tok_rows, top_count, model_width)  16.7 us
  transfers between devices with their start and end apart: 6, of which 4 were waited for; matrix products, arithmetic and copies ran while one was open for 5% of the time, Pallas kernels for 0%

commit v1 on v0

--- a/solution.py
+++ b/solution.py
@@ -8,6 +8,18 @@
 KERNEL = 4
 EPS = 1e-05
 HIGH = lax.Precision.HIGHEST
+
+
+def collect(x, axis, dim):
+    ways, here = (lax.axis_size(axis), lax.axis_index(axis))
+    grown, reach = (x, 1)
+    while reach < ways:
+        theirs = lax.ppermute(grown, axis, [(d, d ^ reach) for d in range(ways)])
+        mine_first = jnp.concatenate([grown, theirs], axis=dim)
+        theirs_first = jnp.concatenate([theirs, grown], axis=dim)
+        grown = jnp.where(here & reach == 0, mine_first, theirs_first)
+        reach = 2 * reach
+    return grown
 
 
 def from_behind(array, axis, by):
@@ -122,11 +134,7 @@
         .reshape(block_len, -1)
         .astype(jnp.bfloat16)
     )
-    partial_out = jnp.dot(
-        normed,
-        lax.all_gather(out_proj, "ctx", axis=1, tiled=True),
-        preferred_element_type=jnp.float32,
-    )
+    partial_out = jnp.dot(normed, collect(out_proj, "ctx", 1), preferred_element_type=jnp.float32)
     mixed = lax.psum_scatter(partial_out, "exp", scatter_dimension=0, tiled=True)
     hidden_f = (residual.astype(jnp.float32) + mixed).astype(jnp.bfloat16).astype(jnp.float32)
     expert_in = (

time: 688 us -> 759 us (1.10)
  blocking collectives: 137 us -> 196 us
    ppermute x0 -> x3, waiting for transfers between devices: none -> 126 us  [collect(): theirs = lax.ppermute(grown, axis, [(d, d ^ reach) for d in range(ways)])]
    all_gather x1 -> x0, waiting for transfers between devices: 74.2 us -> none  [per_device(): lax.all_gather(out_proj, 'ctx', axis=1, tiled=True)]
    all_gather x1, blocking collectives: 10.8 us -> 69.5 us  [carried_in(): everything = jax.tree.map(lambda part: lax.all_gather(part, axis), array)]
    all_gather x1, waiting for transfers between devices: 51.4 us -> 0.01 us  [carried_in(): everything = jax.tree.map(lambda part: lax.all_gather(part, axis), array)]
  transfers between devices with their start and end apart: 6 -> 8, of which waited for: 4 -> 4; matrix products, arithmetic and copies ran while one was open for 5% -> 5% of each run, Pallas kernels for 0% -> 0%
where the time goes in v1:
time: 759 us; the launch traced here: 755 us
  waiting for transfers between devices  256 us (34%)
  local copies, waits for them, and re-layouts  202 us (27%)
  blocking collectives  196 us (26%)
  matrix products  36.1 us (5%)
  other arithmetic  34.1 us (4%)
  starting transfers between devices  16.5 us (2%)
  between operations  13.9 us (2%)
    scatter x1, local copies, waits for them, and re-layouts, per_device(): send_buffer = jnp.zeros((experts, capacity, model_width), jnp.bfloat16).a...  158 us
    all_to_all x1, blocking collectives, per_device(): lax.all_to_all(send_buffer, ('ctx', 'exp'), split_axis=0, concat_axis=0,...  127 us
    ppermute x3, waiting for transfers between devices, collect(): theirs = lax.ppermute(grown, axis, [(d, d ^ reach) for d in range(ways)])  126 us
    all_to_all x1, waiting for transfers between devices, per_device(): lax.all_to_all(finished, ('ctx', 'exp'), split_axis=0, concat_axis=0, til...  120 us
    all_gather x1, blocking collectives, carried_in(): everything = jax.tree.map(lambda part: lax.all_gather(part, axis), array)  69.5 us
    dot_general x1, matrix products, per_device(): jnp.dot(inner, down_weight[0], preferred_element_type=jnp.float32)  18.8 us
    gather x1, local copies, waits for them, and re-layouts, per_device(): returned[flat_ids, slots].reshape(tok_rows, top_count, model_width)  16.7 us
  transfers between devices with their start and end apart: 8, of which 4 were waited for; matrix products, arithmetic and copies ran while one was open for 5% of the time, Pallas kernels for 0%

profile of v1, /device:TPU:13, one launch (start us, length us, event | category | flops | bytes accessed | tf_op | source)
XLA Modules:
  0.0 754.7 jit_solution(3795802522757058981)
XLA Ops:
  6.5 0.7 slice.88
  7.5 3.1 collective-permute-start.1
  10.6 0.7 slice.79
  11.4 3.1 collective-permute-start
  14.5 0.9 slice_convert_fusion.3
  15.4 1.2 reduce-window.14
  17.0 0.9 copy.94
  18.2 0.7 bitcast_convert_fusion.3
  18.9 1.1 copy.98
  20.4 0.8 multiply_convert_fusion.4
  21.4 0.6 multiply_convert_fusion.2
  22.2 1.5 fusion.36
  24.1 20.3 %collective-permute-done.2 = bf16[1024,336]{0,1:T(8,128)(2,1)} collective-permute-done((bf16[1024,336]{0,1:T(8,128)(2,1)S(1)}, bf16[1024,336]{0,1:T(8,128)(2,1)}, u32[]{:S(2)}, u32[]{:S(2)}) %collective-permute-start.2) | collective-permute-done | bytes 688160 | tf_op jit(solution)/shard_map/ppermute | solution.py:17
  44.4 2.4 maximum_select_fusion.3
  47.2 0.7 copy.101
  47.9 0.7 copy.93
  48.6 2.2 copy.107
  50.8 0.7 mul.308
  52.1 69.5 %all_gather.10 = f32[8,2,8]{2,1,0:T(2,128)S(1)} all-gather(f32[1,2,8]{2,1,0:T(2,128)S(1)} %get-tuple-element.171), channel_id=1, replica_groups=mesh['groups'=2,'ctx'=8,'exp'=2] {'ctx'}, dimensions={0}, use_global_device_ids=true | all-gather | bytes 576 | tf_op jit(solution)/shard_map/all_gather | solution.py:33
  122.1 5.2 fusion.30
  127.3 3.8 maximum_select_fusion.2
  131.0 3.8 collective-permute-start.4
  134.9 9.7 %while.16 = (s32[]{:T(128)}, f32[2,8]{1,0:T(2,128)S(1)}, f32[2,8,64,128]{3,2,1,0:T(8,128)S(1)}, s32[]{:T(128)}, f32[8,2,8]{2,1,0:T(2,128)S(1)}, /*index=5*/f32[8,2,8,64,128]{4,3,2,1,0:T(8,128)}, s32[]{:T(128)}, s32[]{:T(128)}) while((s32[]{:T(128)}, f32[2,8]{1,0:T(2,128)S(1)}, f32[2,8,64,128]{3,2,1,0:T(8,128)S(1)}, s32[]{:T(128)}, ...), condition=%wide.region_3.4_spmd.clone, body=%wide.region_2.3_spmd.clone.sunk | while | flops 524340 | bytes 1573299 | solution.py:45
  134.9 1.2 fusion.78
  136.1 1.2 fusion.78
  137.3 1.2 fusion.78
  138.5 1.2 fusion.78
  139.8 1.2 fusion.78
  141.0 1.2 fusion.78
  142.2 1.2 fusion.78
  143.4 1.2 fusion.78
  144.6 2.3 multiply_reduce_fusion.1
  148.0 105.3 %collective-permute-done.4 = bf16[1024,1344]{0,1:T(8,128)(2,1)} collective-permute-done((bf16[1024,1344]{0,1:T(8,128)(2,1)}, bf16[1024,1344]{0,1:T(8,128)(2,1)}, u32[]{:S(2)}, u32[]{:S(2)}) %collective-permute-start.4) | collective-permute-done | bytes 2752544 | tf_op jit(solution)/shard_map/ppermute | solution.py:17
  253.3 8.1 %fusion.1 = f32[256,2688]{1,0:T(8,128)} fusion(bf16[1024,1344]{0,1:T(8,128)(2,1)} %collective-permute-done.4, bf16[1024,1344]{0,1:T(8,128)(2,1)} %maximum_select_fusion.2, pred[]{:T(512)S(6)} %eq.34, f32[256,1024]{1,0:T(8,128)S(1)} %bitcast.126, f32[256,1024]{1,0:T(8,128)S(1)} %copy.106, f32[1024]{0:T(1024)S(1)} %copy-done.12, bf16[256,1024]{1,0:T(8,128)(2,1)} %param.21), kind=kOutput, calls=%fused_computation.10 | convolution fusion | flops 1436418048 | bytes 10883073 | tf_op jit(solution)/shard_map/dot_general | solution.py:137
  262.2 1.7 reduce-window.16
  264.4 10.0 %reduce-scatter.2.cloned.1.call-done = f32[128,2688]{1,0:T(8,128)} async-done(((f32[256,2688]{1,0:T(8,128)}), f32[128,2688]{1,0:T(8,128)}) %reduce-scatter.2.cloned.1.call-update) | async-done | bytes 1376272 | tf_op jit(solution)/shard_map/reduce_scatter | solution.py:138
  274.4 1.6 fusion.26
  276.3 4.9 gather_fusion
  281.1 3.0 broadcast_in_dim.27
  284.1 158.3 %scatter_fusion = bf16[16,64,2688]{2,1,0:T(8,128)(2,1)} fusion(bf16[16,64,2688]{2,1,0:T(8,128)(2,1)} %broadcast_in_dim.27, s32[768]{0:T(1024)S(1)} %get-tuple-element.151, bf16[768,2688]{1,0:T(8,128)(2,1)} %gather_fusion), kind=kCustom, calls=%fused_computation.2 | custom fusion | bytes 12392448 | tf_op jit(solution)/shard_map/scatter | solution.py:160
  442.4 126.7 %all_to_all.10 = bf16[16,64,2688]{2,1,0:T(8,128)(2,1)} all-to-all(bf16[16,64,2688]{2,1,0:T(8,128)(2,1)} %scatter_fusion), channel_id=1, replica_groups=mesh['groups'=2,'ctx'=8,'exp'=2] {'ctx','exp'}, dimensions={0} | all-to-all | bytes 11010048 | tf_op jit(solution)/shard_map/all_to_all | solution.py:162
  569.1 18.8 %convolution_convert_fusion = bf16[1024,2688]{1,0:T(8,128)(2,1)} fusion(bf16[1,928,2688]{2,1,0:T(8,128)(2,1)} %param.35, bf16[1024,2688]{1,0:T(8,128)(2,1)} %bitcast.115, bf16[1,2688,928]{1,2,0:T(8,128)(2,1)} %param.34), kind=kOutput, calls=%fused_computation.8 | convolution fusion | flops 10222927872 | bytes 20987904 | tf_op jit(solution)/shard_map/dot_general | solution.py:167
  587.9 5.6 all-to-all-start.1
  593.7 120.5 %all-to-all-done.1 = bf16[16,64,2688]{2,1,0:T(8,128)(2,1)} async-done(((bf16[16,64,2688]{2,1,0:T(8,128)(2,1)}), bf16[16,64,2688]{2,1,0:T(8,128)(2,1)}, u32[]{:S(2)}, u32[]{:S(2)}) %all-to-all-start.1) | async-done | bytes 5505056 | tf_op jit(solution)/shard_map/all_to_all | solution.py:171
  714.1 16.7 %gather_fusion.1 = bf16[768,2688]{1,0:T(8,128)(2,1)} fusion(bf16[16,64,2688]{2,1,0:T(8,128)(2,1)} %all-to-all-done.1, s32[768]{0:T(1024)S(1)} %get-tuple-element.150), kind=kCustom, calls=%fused_computation.1 | custom fusion | bytes 8263680 | tf_op jit(solution)/shard_map/gather | solution.py:172
  730.8 7.9 %reshape.218 = f32[128,6,2688]{2,1,0:T(8,128)} reshape(bf16[768,2688]{1,0:T(8,128)(2,1)} %gather_fusion.1) | data formatting | bytes 12386304 | tf_op jit(solution)/shard_map/convert_element_type | solution.py:173
  738.7 8.1 %multiply_reduce_fusion = f32[128,2688]{1,0:T(8,128)S(1)} fusion(f32[128,6,2688]{2,1,0:T(8,128)} %reshape.218, f32[128,6]{1,0:T(8,128)S(1)} %copy.109), kind=kLoop, calls=%fused_computation.7 | loop fusion | flops 3784704 | bytes 9636864 | tf_op jit(solution)/shard_map/reduce_sum | solution.py:173
  746.8 1.0 fusion.29
  (94 shorter events, 6.1 us)
Async XLA Ops:
  6.5 8.8 %copy-start = (f32[256,16]{0,1:T(8,128)S(1)}, f32[256,16]{0,1:T(8,128)}, u32[]{:S(2)}) copy-start(f32[256,16]{0,1:T(8,128)} %param.23) | copy-start | bytes 49156
  6.5 14.7 %copy-start.5 = (bf16[256,1024]{1,0:T(8,128)(2,1)S(1)}, bf16[256,1024]{1,0:T(8,128)(2,1)}, u32[]{:S(2)}) copy-start(bf16[256,1024]{1,0:T(8,128)(2,1)} %param.19) | copy-start | bytes 1572868
  6.5 128.3 %all-gather.3.cloned.1.call-start = ((), (), s32[]{:S(2)}) async-start(), calls=%async_computation.4 | async-start | bytes 4718592 | tf_op jit(solution)/shard_map/all_gather | solution.py:33
  7.5 12.7 %collective-permute-start.1 = (bf16[3,2,256]{0,2,1:T(8,128)(2,1)S(1)}, bf16[3,2,256]{0,2,1:T(8,128)(2,1)S(1)}, u32[]{:S(2)}, u32[]{:S(2)}) collective-permute-start(bf16[3,2,256]{0,2,1:T(8,128)(2,1)S(1)} %copy.97), channel_id=1, source_target_pairs={{0,2},{2,4},{4,6},{6,8},{8,10},{10,12},{12,14},{1,3},{3,5},{5,7},{... | collective-permute-start | bytes 9224 | tf_op jit(solution)/shard_map/ppermute | solution.py:28
  11.4 9.8 %collective-permute-start = (bf16[3,1024]{1,0:T(4,128)(2,1)S(1)}, bf16[3,1024]{1,0:T(4,128)(2,1)S(1)}, u32[]{:S(2)}, u32[]{:S(2)}) collective-permute-start(bf16[3,1024]{1,0:T(4,128)(2,1)S(1)} %slice.79), channel_id=1, source_target_pairs={{0,2},{2,4},{4,6},{6,8},{8,10},{10,12},{12,14},{1,3},{3,5},{5,7},{... | collective-permute-start | bytes 18440 | tf_op jit(solution)/shard_map/ppermute | solution.py:28
  21.2 100.4 %copy-start.6 = (bf16[256,1,256]{0,2,1:T(8,128)(2,1)}, bf16[256,1,256]{0,2,1:T(8,128)(2,1)S(1)}, u32[]{:S(2)}) copy-start(bf16[256,1,256]{0,2,1:T(8,128)(2,1)S(1)} %get-tuple-element.172) | copy-start | bytes 393220
  21.4 2.4 copy-start.3
  22.0 28.8 %copy-start.14 = (f32[16]{0:T(128)S(1)}, f32[16]{0:T(128)}, u32[]{:S(2)}) copy-start(f32[16]{0:T(128)} %param.26) | copy-start | bytes 196
  22.0 29.4 %copy-start.13 = (bf16[1024]{0:T(1024)(128)(2,1)S(1)}, bf16[1024]{0:T(1024)(128)(2,1)}, u32[]{:S(2)}) copy-start(bf16[1024]{0:T(1024)(128)(2,1)} %param.28) | copy-start | bytes 6148
  23.7 250.7 %reduce-scatter.2.cloned.1.call-start = ((), (), s32[]{:S(2)}) async-start(), calls=%async_computation.3 | async-start | bytes 4128768 | tf_op jit(solution)/shard_map/reduce_scatter | solution.py:138
  23.8 20.6 %collective-permute-start.2 = (bf16[1024,336]{0,1:T(8,128)(2,1)S(1)}, bf16[1024,336]{0,1:T(8,128)(2,1)}, u32[]{:S(2)}, u32[]{:S(2)}) collective-permute-start(bf16[1024,336]{0,1:T(8,128)(2,1)S(1)} %copy-done.3), channel_id=1, source_target_pairs={{0,2},{2,0},{4,6},{6,4},{8,10},{10,8},{12,14},{14,12},{1,3},{3,1},... | collective-permute-start | bytes 2064392 | tf_op jit(solution)/shard_map/ppermute | solution.py:17
  46.8 80.5 %collective-permute-start.3 = (bf16[1024,672]{0,1:T(8,128)(2,1)S(1)}, bf16[1024,672]{0,1:T(8,128)(2,1)}, u32[]{:S(2)}, u32[]{:S(2)}) collective-permute-start(bf16[1024,672]{0,1:T(8,128)(2,1)S(1)} %maximum_select_fusion.3), channel_id=1, source_target_pairs={{0,4},{2,6},{4,0},{6,2},{8,12},{10,14},{12,8},{14,10},{1,5},{3,7},... | collective-permute-start | bytes 4128776 | tf_op jit(solution)/shard_map/ppermute | solution.py:17
  131.0 13.6 %copy-start.2 = (f32[256,1024]{0,1:T(8,128)S(1)}, f32[256,1024]{0,1:T(8,128)}, u32[]{:S(2)}) copy-start(f32[256,1024]{0,1:T(8,128)} %copy.107) | copy-start | bytes 3145732
  131.0 13.6 %copy-start.7 = (bf16[256,1,256]{0,2,1:T(8,128)(2,1)S(1)}, bf16[256,1,256]{0,2,1:T(8,128)(2,1)}, u32[]{:S(2)}) copy-start(bf16[256,1,256]{0,2,1:T(8,128)(2,1)} %copy-done.6) | copy-start | bytes 393220
  131.0 13.6 %copy-start.8 = (f32[256,2,8]{0,2,1:T(8,128)S(1)}, f32[256,2,8]{0,2,1:T(8,128)}, u32[]{:S(2)}) copy-start(f32[256,2,8]{0,2,1:T(8,128)} %copy.93) | copy-start | bytes 49156
  131.0 13.6 %copy-start.15 = (f32[2,8]{1,0:T(2,128)S(1)}, f32[2,8]{1,0:T(2,128)}, u32[]{:S(2)}) copy-start(f32[2,8]{1,0:T(2,128)} %mul.308) | copy-start | bytes 196
  131.0 122.3 %collective-permute-start.4 = (bf16[1024,1344]{0,1:T(8,128)(2,1)}, bf16[1024,1344]{0,1:T(8,128)(2,1)}, u32[]{:S(2)}, u32[]{:S(2)}) collective-permute-start(bf16[1024,1344]{0,1:T(8,128)(2,1)} %maximum_select_fusion.2), channel_id=1, source_target_pairs={{0,8},{2,10},{4,12},{6,14},{8,0},{10,2},{12,4},{14,6},{1,9},{3,11}... | collective-permute-start | bytes 8257544 | tf_op jit(solution)/shard_map/ppermute | solution.py:17
  146.9 106.4 %copy-start.12 = (f32[1024]{0:T(1024)S(1)}, f32[1024]{0:T(1024)}, u32[]{:S(2)}) copy-start(f32[1024]{0:T(1024)} %convert_element_type.82) | copy-start | bytes 12292
  253.3 8.2 %copy-start.10 = (s32[128,6]{0,1:T(8,128)S(1)}, s32[128,6]{0,1:T(8,128)}, u32[]{:S(2)}) copy-start(s32[128,6]{0,1:T(8,128)} %param.32) | copy-start | bytes 9220
  253.3 8.7 %copy-start.9 = (bf16[2688]{0:T(1024)(128)(2,1)S(1)}, bf16[2688]{0:T(1024)(128)(2,1)}, u32[]{:S(2)}) copy-start(bf16[2688]{0:T(1024)(128)(2,1)} %param.31) | copy-start | bytes 16132
  253.3 21.1 %copy-start.4 = (bf16[128,2688]{1,0:T(8,128)(2,1)S(1)}, bf16[128,2688]{1,0:T(8,128)(2,1)}, u32[]{:S(2)}) copy-start(bf16[128,2688]{1,0:T(8,128)(2,1)} %param.30) | copy-start | bytes 2064388
  587.9 5.6 copy-start.11
  587.9 126.2 %all-to-all-start.1 = ((bf16[16,64,2688]{2,1,0:T(8,128)(2,1)}), bf16[16,64,2688]{2,1,0:T(8,128)(2,1)}, u32[]{:S(2)}, u32[]{:S(2)}) async-start(bf16[16,64,2688]{2,1,0:T(8,128)(2,1)} %bitcast.114), calls=%async_computation.2 | async-start | bytes 11010048 | tf_op jit(solution)/shard_map/all_to_all | solution.py:171
  738.7 9.1 %copy-start.1 = (f32[256,16]{0,1:T(8,128)S(1)}, f32[256,16]{0,1:T(8,128)}, u32[]{:S(2)}) copy-start(f32[256,16]{0,1:T(8,128)} %param.23) | copy-start | bytes 49156
Sparse Core Ops, SparseCore 0:
  23.8 94.2 all-gather.2
  261.6 12.7 reduce-scatter.1
